TPU v7x, 32 devices: a whole 2x2x4 slice. The times are simulated.
32 devices in a mesh: mpo: 4 (over x, core), bond: 8 (over z, y).
Axes of the slice: x: 2, y: 2, z: 4, core: 2. Of those that a mesh axis runs over, the one named last changes fastest.
Arguments:
- environment: bfloat16 [4096, 40, 4096], P(None, 'mpo', 'bond'), may hold values from -60 to 60
- site_tensor: bfloat16 [4096, 4, 4096], P('bond'), may hold values from -0.09375 to 0.09375
- mpo_tensor: bfloat16 [40, 40, 4, 4], replicated, may hold values from -0.5 to 0.5
- sketch_site: bfloat16 [4096, 128], replicated, may hold values from -6 to 6
- sketch_expand: bfloat16 [128, 40, 4096], P('mpo'), may hold values from -60 to 60
- row_sectors: int32 [2, 4096, 4], P(None, 'bond'), may hold values from 0 to 5, as said below
- column_sectors: int32 [2, 128], replicated, may hold values from 0 to 5, as said below
Outputs:
- basis: bfloat16 [4096, 4, 128], P('bond')
- extended: float32 [128, 40, 128], P('bond', 'mpo')
Inputs may be any that keep to these rules, and one draw needn't show every extreme that they name: `row_sectors`: every joined row's label pair is (4, 0) or (5, 1); the rows labelled (5, 1) are one run of 64 consecutive joined rows (a, s) in the order a then s. `column_sectors`: every column's label pair is (4, 0) or (5, 1); exactly 16 columns are labelled (5, 1).
All inputs are finite; a program needn't handle non-finite values.
Results may differ from a plain program's by a relative error of at most 0.0064.
Values may be sent and summed in bfloat16 or wider, within the bound.
A program may use at most 128 MiB of HBM per device.

v0:
```python
import jax
import jax.numpy as jnp
from jax import lax
from jax.sharding import PartitionSpec as P

mixing = 0.5
shift_tolerance = 1e-06


def sector_mask(row_labels, column_labels):
    match = (row_labels[0][:, :, None] == column_labels[0][None, None, :]) & (
        row_labels[1][:, :, None] == column_labels[1][None, None, :]
    )
    return match.astype(jnp.float32)


def gram_of(left, right):
    column_count = left.shape[-1]
    return jnp.dot(
        left.reshape(-1, column_count).T,
        right.reshape(-1, column_count),
        precision=lax.Precision.HIGHEST,
        preferred_element_type=jnp.float32,
    )


def orthonormal(factor, values):
    column_count = values.shape[-1]
    solved = jax.scipy.linalg.solve_triangular(
        factor, values.reshape(-1, column_count).T, lower=True
    )
    return solved.T.reshape(values.shape).astype(jnp.bfloat16)


def body(
    environment, site_tensor, mpo_tensor, sketch_site, sketch_expand, row_sectors, column_sectors
):
    mpo_index = lax.axis_index("mpo")
    mpo_count = lax.axis_size("mpo")
    physical_width = environment.shape[1]
    local_rows = site_tensor.shape[0]
    physical = site_tensor.shape[1]
    column_count = column_sectors.shape[1]
    operator_rows = lax.dynamic_slice_in_dim(
        mpo_tensor, mpo_index * physical_width, physical_width, 0
    )
    sketched = jnp.einsum(
        "asb,kwb->wska", site_tensor, sketch_expand, preferred_element_type=jnp.float32
    ).astype(jnp.bfloat16)
    applied = jnp.einsum(
        "vwst,wtka->vska", mpo_tensor, sketched, preferred_element_type=jnp.float32
    ).astype(jnp.bfloat16)
    contracted = lax.all_to_all(applied, "mpo", split_axis=0, concat_axis=2, tiled=True)
    env_rows = environment
    expand_part = lax.psum_scatter(
        jnp.einsum("awc,wskc->ask", env_rows, contracted, preferred_element_type=jnp.float32),
        "bond",
        scatter_dimension=0,
        tiled=True,
    )
    mask_rows = sector_mask(row_sectors, column_sectors)
    share = local_rows // mpo_count
    offset = mpo_index * share
    expand_whole = lax.psum(expand_part, "mpo") * mask_rows
    site_whole = (
        jnp.dot(
            site_tensor.reshape(local_rows * physical, -1),
            sketch_site,
            preferred_element_type=jnp.float32,
        ).reshape(local_rows, physical, column_count)
        * mask_rows
    )
    part_site = lax.dynamic_slice_in_dim(site_whole, offset, share, 0)
    expansion_piece = lax.dynamic_slice_in_dim(expand_whole, offset, share, 0)
    square_site, square_expand = lax.psum(
        (jnp.sum(part_site * part_site), jnp.sum(expansion_piece * expansion_piece)),
        ("mpo", "bond"),
    )
    mix = mixing * jnp.sqrt((square_site + shift_tolerance) / (square_expand + shift_tolerance))
    combo_part = part_site + mix * expansion_piece
    gram_total = lax.psum(gram_of(combo_part, combo_part), ("mpo", "bond"))
    factor = jnp.linalg.cholesky(gram_total)
    basis_local = orthonormal(factor, site_whole + mix * expand_whole)
    flat_basis = basis_local.reshape(local_rows, physical * column_count)
    piece = lax.all_gather(basis_local, "bond", axis=0, tiled=True)
    env_rows = environment
    projected = jnp.einsum(
        "ax,awc->wxc",
        piece.reshape(piece.shape[0], -1),
        env_rows,
        preferred_element_type=jnp.float32,
    ).astype(jnp.bfloat16)
    couple_merged = jnp.einsum(
        "wxc,cy->wxy", projected, flat_basis, preferred_element_type=jnp.float32
    ).reshape(physical_width, physical, column_count, physical, column_count)
    boundary_share = jnp.einsum(
        "wvst,wsktl->kvl",
        operator_rows.astype(jnp.float32),
        couple_merged,
        precision=lax.Precision.HIGHEST,
    )
    reduced = lax.psum_scatter(boundary_share, "bond", scatter_dimension=0, tiled=True)
    extended = lax.psum_scatter(reduced, "mpo", scatter_dimension=1, tiled=True)
    return (basis_local, extended)


def solution(mesh):
    placed = (
        P(None, "mpo", "bond"),
        P("bond", None, None),
        P(),
        P(),
        P("mpo", None, None),
        P(None, "bond", None),
        P(),
    )
    return jax.shard_map(
        body,
        mesh=mesh,
        in_specs=placed,
        out_specs=(P("bond", None, None), P("bond", "mpo", None)),
        check_vma=False,
    )
```

profile of v0, /device:TPU:0, one launch (start us, length us, event | category | flops | bytes accessed | tf_op | source)
XLA Modules:
  0.0 739.9 jit_solution(15109001147891510651)
XLA Ops:
  7.2 31.3 %fusion.4 = bf16[32,40,512,4]{2,1,3,0:T(8,128)(2,1)} fusion(bf16[512,4,4096]{2,1,0:T(4,128)(2,1)} %param.8, bf16[32,40,4096]{2,1,0:T(8,128)(2,1)} %param.11), kind=kOutput, calls=%fused_computation.4 | convolution fusion | flops 21474836480 | bytes 32505856 | tf_op jit(solution)/shard_map/asb,kwb->wska/dot_general | solution.py:47
  38.5 4.6 fusion.13
  43.1 2.7 copy.35
  45.8 63.4 %all_to_all.18 = bf16[40,4,32,512]{3,1,2,0:T(4,128)(2,1)S(1)} all-to-all(bf16[40,4,32,512]{3,1,2,0:T(4,128)(2,1)S(1)} %copy.35), channel_id=1, replica_groups=mesh['mpo'=4,'bond'=8] {'mpo'}, dimensions={0} | all-to-all | bytes 10485760 | tf_op jit(solution)/shard_map/all_to_all | solution.py:53
  109.2 1.7 copy.36
  110.9 0.6 copy.37
  111.6 27.7 %fusion.10 = f32[4096,4,128]{2,0,1:T(8,128)} fusion(bf16[10,4,128,512]{3,2,0,1:T(8,128)(2,1)S(1)} %bitcast.100, bf16[4096,10,512]{2,0,1:T(8,128)(2,1)} %param.7), kind=kOutput, calls=%fused_computation.11 | convolution fusion | flops 21474836480 | bytes 55574528 | tf_op jit(solution)/shard_map/awc,wskc->ask/dot_general | solution.py:56
  139.4 148.3 %reduce-scatter.4.cloned.1.call-done = f32[512,4,128]{2,0,1:T(8,128)} async-done(((f32[4096,4,128]{2,0,1:T(8,128)}), f32[512,4,128]{2,0,1:T(8,128)}) %reduce-scatter.4.cloned.1.call-update) | async-done | bytes 1048592 | tf_op jit(solution)/shard_map/reduce_scatter | solution.py:55
  287.8 30.4 %fusion.22 = f32[512,4,128]{2,0,1:T(8,128)S(1)} fusion(bf16[512,4,4096]{2,1,0:T(4,128)(2,1)} %param.8, bf16[4096,128]{1,0:T(8,128)(2,1)S(1)} %copy-done, s32[128]{0:T(128)S(1)} %get-tuple-element.13, s32[512,4]{0,1:T(4,128)S(1)} %get-tuple-element.11, s32[128]{0:T(128)S(1)} %get-tuple-element.12, s32[512,4]{0,1:T(4,128)S(1)} %get-tuple-element.10), kind=kOutput, calls=%fused_computation.18 | convolution fusion | flops 2148532224 | bytes 18891776 | tf_op jit(solution)/shard_map/dot_general | solution.py:66
  318.2 0.7 multiply_reduce_fusion.1
  318.9 6.6 all-reduce.4.cloned.1.call-done
  325.5 1.8 fusion.28
  327.2 0.7 multiply_reduce_fusion
  327.9 40.0 %all-reduce = (f32[]{:T(128)}, f32[]{:T(128)}) all-reduce(f32[]{:T(128)} %multiply_reduce_fusion.1, f32[]{:T(128)} %multiply_reduce_fusion), channel_id=1, replica_groups=mesh['mpo'=4,'bond'=8] {'mpo','bond'}, use_global_device_ids=true, to_apply=%region_1.0 | all-reduce | flops 2 | bytes 16 | tf_op jit(solution)/shard_map/psum | solution.py:75
  369.3 1.2 convolution_bitcast_fusion
  370.6 0.2 all-gather.2.cloned.1.call-start
  370.8 119.7 %all-reduce.6.cloned.1.call-done = f32[128,128]{0,1:T(8,128)} async-done(((f32[128,128]{0,1:T(8,128)}), f32[128,128]{0,1:T(8,128)}) %all-reduce.6.cloned.1.call-update) | async-done | bytes 65552 | tf_op jit(solution)/shard_map/psum | solution.py:81
  490.5 0.9 copy.41
  491.4 0.9 fusion.41
  492.3 11.7 %cholesky.16 = f32[128,128]{1,0:T(8,128)S(1)} custom-call(f32[128,128]{1,0:T(8,128)S(1)} %fusion.41), custom_call_target="Cholesky" | custom-call | tf_op jit(solution)/shard_map/jit(cholesky)/cholesky | solution.py:82
  504.0 0.6 compare_reduce_fusion
  504.7 0.7 fusion.38
  505.4 9.8 %custom-call.7 = f32[1,128,128]{1,2,0:T(8,128)S(1)} custom-call(f32[1,128,128]{2,1,0:T(8,128)S(1)} %fusion.38), custom_call_target="InvertDiagBlocksLowerTriangular" | custom-call | tf_op jit(solution)/shard_map/jit(_solve_triangular)/triangular_solve | solution.py:29
  515.2 2.0 convolution_convert_fusion.1
  517.3 75.9 %all-gather.2.cloned.1.call-done = bf16[4096,4,128]{0,2,1:T(8,128)(2,1)} async-done(((bf16[512,4,128]{0,2,1:T(8,128)(2,1)}), bf16[4096,4,128]{0,2,1:T(8,128)(2,1)}) %all-gather.2.cloned.1.call-update) | async-done | bytes 4194320 | tf_op jit(solution)/shard_map/all_gather | solution.py:85
  593.2 27.9 %convolution_convert_fusion = bf16[512,10,512]{2,0,1:T(8,128)(2,1)S(1)} fusion(bf16[4096,512,1]{0,1,2:T(8,128)(2,1)} %bitcast.101, bf16[4096,10,512]{2,0,1:T(8,128)(2,1)} %param.7), kind=kOutput, calls=%fused_computation.16 | convolution fusion | flops 21477457920 | bytes 51380224 | tf_op jit(solution)/shard_map/ax,awc->wxc/dot_general | solution.py:87
  621.1 2.9 fusion.29
  624.0 16.9 %fusion.19 = f32[128,40,128]{2,1,0:T(8,128)} fusion(f32[10,4,128,4,128]{4,2,3,1,0:T(8,128)S(1)} %fusion.29, bf16[40,40,4,4]{1,0,3,2:T(8,128)(2,1)S(1)} %copy.34, s32[]{:T(128)S(6)} %select_n.13), kind=kOutput, calls=%fused_computation.17 | convolution fusion | flops 1258291200 | bytes 13172740 | tf_op jit(solution)/shard_map/wvst,wsktl->kvl/dot_general | solution.py:96
  640.9 69.2 %reduce-scatter.6.cloned.1.call-done = f32[16,40,128]{2,1,0:T(8,128)} async-done(((f32[128,40,128]{2,1,0:T(8,128)}), f32[16,40,128]{2,1,0:T(8,128)}) %reduce-scatter.6.cloned.1.call-update) | async-done | bytes 327696 | tf_op jit(solution)/shard_map/reduce_scatter | solution.py:102
  710.2 1.7 copy.45
  711.9 1.1 copy.46
  713.0 19.7 %reduce-scatter.8.cloned.1.call-done = f32[16,10,128]{2,0,1:T(8,128)} async-done(((f32[16,40,128]{2,0,1:T(8,128)}), f32[16,10,128]{2,0,1:T(8,128)}) %reduce-scatter.8.cloned.1.call-update) | async-done | bytes 81936 | tf_op jit(solution)/shard_map/reduce_scatter | solution.py:103
  (25 shorter events, 0.4 us)
Async XLA Ops:
  7.2 280.6 %copy-start = (bf16[4096,128]{1,0:T(8,128)(2,1)S(1)}, bf16[4096,128]{1,0:T(8,128)(2,1)}, u32[]{:S(2)}) copy-start(bf16[4096,128]{1,0:T(8,128)(2,1)} %param.10) | copy-start | bytes 3145732
  7.2 31.4 %copy-start.2 = (bf16[40,40,4,4]{1,3,2,0:T(4,128)(2,1)S(1)}, bf16[40,40,4,4]{1,3,2,0:T(4,128)(2,1)}, u32[]{:S(2)}) copy-start(bf16[40,40,4,4]{1,3,2,0:T(4,128)(2,1)} %param.9) | copy-start | bytes 153604
  7.2 280.5 %reduce-scatter.4.cloned.1.call-start = ((), (), s32[]{:S(2)}) async-start(), calls=%async_computation.4 | async-start | bytes 9437184 | tf_op jit(solution)/shard_map/reduce_scatter | solution.py:55
  111.6 27.8 %copy-start.4 = (s32[2,128]{1,0:T(2,128)S(1)}, s32[2,128]{1,0:T(2,128)}, u32[]{:S(2)}) copy-start(s32[2,128]{1,0:T(2,128)} %param.13) | copy-start | bytes 3076
  111.6 27.8 %copy-start.3 = (s32[2,512,4]{1,2,0:T(4,128)S(1)}, s32[2,512,4]{1,2,0:T(4,128)}, u32[]{:S(2)}) copy-start(s32[2,512,4]{1,2,0:T(4,128)} %param.12) | copy-start | bytes 49156
  139.3 186.1 %all-reduce.4.cloned.1.call-start = ((), (), s32[]{:S(2)}) async-start(), calls=%async_computation.5 | async-start | bytes 2097152 | tf_op jit(solution)/shard_map/psum | solution.py:64
  287.7 202.8 %all-reduce.6.cloned.1.call-start = ((), (), s32[]{:S(2)}) async-start(), calls=%async_computation.6 | async-start | bytes 131072 | tf_op jit(solution)/shard_map/psum | solution.py:81
  370.6 222.6 %all-gather.2.cloned.1.call-start = ((), (), s32[]{:S(2)}) async-start(), calls=%async_computation.7 | async-start | bytes 4718592 | tf_op jit(solution)/shard_map/all_gather | solution.py:85
  517.2 193.0 %reduce-scatter.6.cloned.1.call-start = ((), (), s32[]{:S(2)}) async-start(), calls=%async_computation.8 | async-start | bytes 2949120 | tf_op jit(solution)/shard_map/reduce_scatter | solution.py:102
  593.2 27.9 %copy-start.1 = (bf16[512,4,128]{0,2,1:T(8,128)(2,1)S(1)}, bf16[512,4,128]{0,2,1:T(8,128)(2,1)}, u32[]{:S(2)}) copy-start(bf16[512,4,128]{0,2,1:T(8,128)(2,1)} %convolution_convert_fusion.1) | copy-start | bytes 1572868
  640.9 91.8 %reduce-scatter.8.cloned.1.call-start = ((), (), s32[]{:S(2)}) async-start(), calls=%async_computation.9 | async-start | bytes 409600 | tf_op jit(solution)/shard_map/reduce_scatter | solution.py:103
Sparse Core Ops, SparseCore 0:
  139.5 148.2 reduce-scatter.3
  290.1 35.3 all-reduce.3
  370.7 119.7 all-reduce.5
  517.3 75.8 all-gather.1
  641.0 69.0 reduce-scatter.5
  713.1 19.5 reduce-scatter.7
where the time goes:
time: 749 us; the launch traced here: 740 us
  waiting for transfers between devices  439 us (59%)
  matrix products  145 us (19%)
  blocking collectives  103 us (14%)
  other arithmetic  26.8 us (4%)
  between operations  16.1 us (2%)
  local copies, waits for them, and re-layouts  8.83 us (1%)
    reduce_scatter x1, waiting for transfers between devices, body(): lax.psum_scatter(jnp.einsum('awc,wskc->ask', env_rows, contracted, prefer...  148 us
    psum x1, waiting for transfers between devices, body(): gram_total = lax.psum(gram_of(combo_part, combo_part), ('mpo', 'bond'))  120 us
    all_gather x1, waiting for transfers between devices, body(): piece = lax.all_gather(basis_local, 'bond', axis=0, tiled=True)  75.9 us
    reduce_scatter x1, waiting for transfers between devices, body(): lax.psum_scatter(boundary_share, 'bond', scatter_dimension=0, tiled=True)  69.2 us
    all_to_all x1, blocking collectives, body(): lax.all_to_all(applied, 'mpo', split_axis=0, concat_axis=2, tiled=True)  63.4 us
    psum x1, blocking collectives, body(): lax.psum((jnp.sum(part_site * part_site), jnp.sum(expansion_piece * expan...  40 us
    dot_general x1, matrix products, body(): jnp.einsum('asb,kwb->wska', site_tensor, sketch_expand, preferred_element...  31.3 us
    dot_general x1, matrix products, body(): jnp.dot(site_tensor.reshape(local_rows * physical, -1), sketch_site, pref...  30.4 us
  transfers between devices with their start and end apart: 6, of which 6 were waited for; matrix products, arithmetic and copies ran while one was open for 4% of the time, Pallas kernels for 0%

commit v1 on v0

--- a/solution.py
+++ b/solution.py
@@ -50,7 +50,10 @@
     applied = jnp.einsum(
         "vwst,wtka->vska", mpo_tensor, sketched, preferred_element_type=jnp.float32
     ).astype(jnp.bfloat16)
-    contracted = lax.all_to_all(applied, "mpo", split_axis=0, concat_axis=2, tiled=True)
+    contracted = jnp.concatenate(
+        lax.all_to_all(jnp.stack(jnp.split(applied, lax.axis_size("mpo"), axis=0)), "mpo", 0, 0),
+        axis=2,
+    )
     env_rows = environment
     expand_part = lax.psum_scatter(
         jnp.einsum("awc,wskc->ask", env_rows, contracted, preferred_element_type=jnp.float32),

time: 749 us -> 753 us (level)
  no operation moved by 1% of the time
where the time goes in v1:
time: 753 us; the launch traced here: 744 us
  waiting for transfers between devices  439 us (58%)
  matrix products  145 us (19%)
  blocking collectives  103 us (14%)
  other arithmetic  28.4 us (4%)
  between operations  16.1 us (2%)
  local copies, waits for them, and re-layouts  11.5 us (2%)
    reduce_scatter x1, waiting for transfers between devices, body(): lax.psum_scatter(jnp.einsum('awc,wskc->ask', env_rows, contracted, prefer...  148 us
    psum x1, waiting for transfers between devices, body(): gram_total = lax.psum(gram_of(combo_part, combo_part), ('mpo', 'bond'))  120 us
    all_gather x1, waiting for transfers between devices, body(): piece = lax.all_gather(basis_local, 'bond', axis=0, tiled=True)  75.9 us
    reduce_scatter x1, waiting for transfers between devices, body(): lax.psum_scatter(boundary_share, 'bond', scatter_dimension=0, tiled=True)  69.4 us
    all_to_all x1, blocking collectives, body(): lax.all_to_all(jnp.stack(jnp.split(applied, lax.axis_size('mpo'), axis=0)...  63.4 us
    psum x1, blocking collectives, body(): lax.psum((jnp.sum(part_site * part_site), jnp.sum(expansion_piece * expan...  40 us
    dot_general x1, matrix products, body(): jnp.einsum('asb,kwb->wska', site_tensor, sketch_expand, preferred_element...  31.3 us
    dot_general x1, matrix products, body(): jnp.dot(site_tensor.reshape(local_rows * physical, -1), sketch_site, pref...  30.4 us
  transfers between devices with their start and end apart: 6, of which 6 were waited for; matrix products, arithmetic and copies ran while one was open for 4% of the time, Pallas kernels for 0%

profile of v1, /device:TPU:0, one launch (start us, length us, event | category | flops | bytes accessed | tf_op | source)
XLA Modules:
  0.0 743.8 jit_solution(2658797177516635998)
XLA Ops:
  7.2 31.3 %fusion.4 = bf16[32,40,512,4]{2,1,3,0:T(8,128)(2,1)} fusion(bf16[512,4,4096,1]{2,1,0,3:T(4,128)(2,1)} %bitcast.105, bf16[32,40,4096]{2,1,0:T(8,128)(2,1)} %param.11), kind=kOutput, calls=%fused_computation.4 | convolution fusion | flops 21474836480 | bytes 32505856 | tf_op jit(solution)/shard_map/asb,kwb->wska/dot_general | solution.py:47
  38.6 4.6 fusion.12
  43.2 3.4 slice_bitcast_fusion.3
  46.6 1.6 pad_maximum_fusion
  48.2 3.0 copy.22
  51.2 63.4 %all_to_all.5 = bf16[4,10,4,32,512]{4,3,2,1,0:T(8,128)(2,1)S(1)} all-to-all(bf16[4,10,4,32,512]{4,3,2,1,0:T(8,128)(2,1)S(1)} %copy.22), channel_id=1, replica_groups=mesh['mpo'=4,'bond'=8] {'mpo'}, dimensions={0} | all-to-all | bytes 10485760 | tf_op jit(solution)/shard_map/all_to_all | solution.py:54
  114.6 0.6 copy.23
  115.2 27.7 %fusion.9 = f32[4096,4,128]{2,0,1:T(8,128)} fusion(bf16[10,4,128,512]{3,2,0,1:T(8,128)(2,1)S(1)} %bitcast.104, bf16[4096,10,512]{2,0,1:T(8,128)(2,1)} %param.7), kind=kOutput, calls=%fused_computation.11 | convolution fusion | flops 21474836480 | bytes 55574528 | tf_op jit(solution)/shard_map/awc,wskc->ask/dot_general | solution.py:59
  143.7 147.7 %reduce-scatter.4.cloned.1.call-done = f32[512,4,128]{2,0,1:T(8,128)} async-done(((f32[4096,4,128]{2,0,1:T(8,128)}), f32[512,4,128]{2,0,1:T(8,128)}) %reduce-scatter.4.cloned.1.call-update) | async-done | bytes 1048592 | tf_op jit(solution)/shard_map/reduce_scatter | solution.py:58
  291.4 30.4 %fusion.21 = f32[512,4,128]{2,0,1:T(8,128)S(1)} fusion(bf16[512,4,4096]{2,1,0:T(4,128)(2,1)} %param.8, bf16[4096,128]{1,0:T(8,128)(2,1)S(1)} %copy-done, s32[128]{0:T(128)S(1)} %get-tuple-element.15, s32[512,4]{0,1:T(4,128)S(1)} %get-tuple-element.13, s32[128]{0:T(128)S(1)} %get-tuple-element.14, s32[512,4]{0,1:T(4,128)S(1)} %get-tuple-element.12), kind=kOutput, calls=%fused_computation.22 | convolution fusion | flops 2148532224 | bytes 18891776 | tf_op jit(solution)/shard_map/dot_general | solution.py:69
  321.8 0.7 multiply_reduce_fusion.1
  322.5 6.6 all-reduce.4.cloned.1.call-done
  329.1 1.8 fusion.27
  330.9 0.7 multiply_reduce_fusion
  331.6 40.0 %all-reduce = (f32[]{:T(128)}, f32[]{:T(128)}) all-reduce(f32[]{:T(128)} %multiply_reduce_fusion.1, f32[]{:T(128)} %multiply_reduce_fusion), channel_id=1, replica_groups=mesh['mpo'=4,'bond'=8] {'mpo','bond'}, use_global_device_ids=true, to_apply=%region_1.0 | all-reduce | flops 2 | bytes 16 | tf_op jit(solution)/shard_map/psum | solution.py:78
  373.0 1.2 convolution_bitcast_fusion
  374.4 119.7 %all-reduce.6.cloned.1.call-done = f32[128,128]{0,1:T(8,128)} async-done(((f32[128,128]{0,1:T(8,128)}), f32[128,128]{0,1:T(8,128)}) %all-reduce.6.cloned.1.call-update) | async-done | bytes 65552 | tf_op jit(solution)/shard_map/psum | solution.py:84
  494.2 0.9 copy.27
  495.1 0.9 fusion.40
  496.0 11.7 %cholesky.16 = f32[128,128]{1,0:T(8,128)S(1)} custom-call(f32[128,128]{1,0:T(8,128)S(1)} %fusion.40), custom_call_target="Cholesky" | custom-call | tf_op jit(solution)/shard_map/jit(cholesky)/cholesky | solution.py:85
  507.7 0.6 compare_reduce_fusion
  508.4 0.7 fusion.37
  509.0 9.8 %custom-call.7 = f32[1,128,128]{1,2,0:T(8,128)S(1)} custom-call(f32[1,128,128]{2,1,0:T(8,128)S(1)} %fusion.37), custom_call_target="InvertDiagBlocksLowerTriangular" | custom-call | tf_op jit(solution)/shard_map/jit(_solve_triangular)/triangular_solve | solution.py:29
  518.8 2.0 convolution_convert_fusion.1
  520.9 75.9 %all-gather.2.cloned.1.call-done = bf16[4096,4,128]{0,2,1:T(8,128)(2,1)} async-done(((bf16[512,4,128]{0,2,1:T(8,128)(2,1)}), bf16[4096,4,128]{0,2,1:T(8,128)(2,1)}) %all-gather.2.cloned.1.call-update) | async-done | bytes 4194320 | tf_op jit(solution)/shard_map/all_gather | solution.py:88
  596.9 27.9 %convolution_convert_fusion = bf16[512,10,512]{2,0,1:T(8,128)(2,1)S(1)} fusion(bf16[4096,512,1]{0,1,2:T(8,128)(2,1)} %bitcast.106, bf16[4096,10,512]{2,0,1:T(8,128)(2,1)} %param.7), kind=kOutput, calls=%fused_computation.16 | convolution fusion | flops 21477457920 | bytes 51380224 | tf_op jit(solution)/shard_map/ax,awc->wxc/dot_general | solution.py:90
  624.8 2.9 fusion.28
  627.7 16.9 %fusion.18 = f32[128,40,128]{2,1,0:T(8,128)} fusion(f32[10,4,128,4,128]{4,2,3,1,0:T(8,128)S(1)} %fusion.28, bf16[40,40,4,4]{1,0,3,2:T(8,128)(2,1)S(1)} %copy.21, s32[]{:T(128)S(6)} %select_n.13), kind=kOutput, calls=%fused_computation.21 | convolution fusion | flops 1258291200 | bytes 13172740 | tf_op jit(solution)/shard_map/wvst,wsktl->kvl/dot_general | solution.py:99
  644.6 69.4 %reduce-scatter.6.cloned.1.call-done = f32[16,40,128]{2,1,0:T(8,128)} async-done(((f32[128,40,128]{2,1,0:T(8,128)}), f32[16,40,128]{2,1,0:T(8,128)}) %reduce-scatter.6.cloned.1.call-update) | async-done | bytes 327696 | tf_op jit(solution)/shard_map/reduce_scatter | solution.py:105
  714.0 1.7 copy.30
  715.8 1.1 copy.31
  716.8 19.7 %reduce-scatter.8.cloned.1.call-done = f32[16,10,128]{2,0,1:T(8,128)} async-done(((f32[16,40,128]{2,0,1:T(8,128)}), f32[16,10,128]{2,0,1:T(8,128)}) %reduce-scatter.8.cloned.1.call-update) | async-done | bytes 81936 | tf_op jit(solution)/shard_map/reduce_scatter | solution.py:106
  (26 shorter events, 1.3 us)
Async XLA Ops:
  7.2 284.3 %copy-start = (bf16[4096,128]{1,0:T(8,128)(2,1)S(1)}, bf16[4096,128]{1,0:T(8,128)(2,1)}, u32[]{:S(2)}) copy-start(bf16[4096,128]{1,0:T(8,128)(2,1)} %param.10) | copy-start | bytes 3145732
  7.2 284.2 %reduce-scatter.4.cloned.1.call-start = ((), (), s32[]{:S(2)}) async-start(), calls=%async_computation.4 | async-start | bytes 9437184 | tf_op jit(solution)/shard_map/reduce_scatter | solution.py:58
  7.2 31.4 %copy-start.2 = (bf16[40,40,4,4]{1,3,2,0:T(4,128)(2,1)S(1)}, bf16[40,40,4,4]{1,3,2,0:T(4,128)(2,1)}, u32[]{:S(2)}) copy-start(bf16[40,40,4,4]{1,3,2,0:T(4,128)(2,1)} %param.9) | copy-start | bytes 153604
  143.0 0.7 copy-start.4
  143.0 0.7 copy-start.3
  143.0 186.1 %all-reduce.4.cloned.1.call-start = ((), (), s32[]{:S(2)}) async-start(), calls=%async_computation.5 | async-start | bytes 2097152 | tf_op jit(solution)/shard_map/psum | solution.py:67
  291.4 202.8 %all-reduce.6.cloned.1.call-start = ((), (), s32[]{:S(2)}) async-start(), calls=%async_computation.6 | async-start | bytes 131072 | tf_op jit(solution)/shard_map/psum | solution.py:84
  374.2 222.6 %all-gather.2.cloned.1.call-start = ((), (), s32[]{:S(2)}) async-start(), calls=%async_computation.7 | async-start | bytes 4718592 | tf_op jit(solution)/shard_map/all_gather | solution.py:88
  520.8 193.2 %reduce-scatter.6.cloned.1.call-start = ((), (), s32[]{:S(2)}) async-start(), calls=%async_computation.8 | async-start | bytes 2949120 | tf_op jit(solution)/shard_map/reduce_scatter | solution.py:105
  596.9 27.9 %copy-start.1 = (bf16[512,4,128]{0,2,1:T(8,128)(2,1)S(1)}, bf16[512,4,128]{0,2,1:T(8,128)(2,1)}, u32[]{:S(2)}) copy-start(bf16[512,4,128]{0,2,1:T(8,128)(2,1)} %convolution_convert_fusion.1) | copy-start | bytes 1572868
  644.6 91.9 %reduce-scatter.8.cloned.1.call-start = ((), (), s32[]{:S(2)}) async-start(), calls=%async_computation.9 | async-start | bytes 409600 | tf_op jit(solution)/shard_map/reduce_scatter | solution.py:106
Sparse Core Ops, SparseCore 0:
  143.1 148.2 reduce-scatter.3
  293.7 35.3 all-reduce.3
  374.3 119.7 all-reduce.5
  521.0 75.8 all-gather.1
  644.7 69.2 reduce-scatter.5
  716.9 19.5 reduce-scatter.7
